TPU v7x, 256 devices: a whole 4x4x8 slice. The times are simulated.
256 devices in a mesh: row: 8 (over y, core), col: 32 (over x, z).
Axes of the slice: x: 4, y: 4, z: 8, core: 2. Of those that a mesh axis runs over, the one named last changes fastest.
Arguments:
- stored: float32 [20, 8, 128, 5, 32, 128], P(None, 'row', None, None, 'col'), may hold values from -1 to 13
- rhs: float32 [5, 32, 128, 128], P(None, 'col'), may hold values from -60 to 60
Outputs:
- solution: float32 [5, 32, 128, 128], P(None, 'col')
- residual: float32 [5, 32, 128, 128], P(None, 'col')
All inputs are finite; a program needn't handle non-finite values.
Results may differ from a plain program's by a relative error of at most 0.0003.
Values sent between devices are 32-bit elements; how exact they have to be, the bound alone decides.
A program may use at most 128 MiB of HBM per device.

v0:
```python
import jax
import jax.numpy as jnp
from jax import lax
from jax.sharding import PartitionSpec as P

ITERS = 2
HIGHEST = lax.Precision.HIGHEST


def partner_2(value, axis, distance):
    mask = 2**distance
    pairs = [(source, source ^ mask) for source in range(lax.axis_size(axis))]
    return lax.ppermute(value, axis, pairs)


def spread(value, axis, source):
    kept = jnp.where(lax.axis_index(axis) == source, value, 0).astype(value.dtype)
    return lax.psum(kept, axis)


def gram_local(left_side, right_side):
    columns_n = left_side.shape[-1]
    return jnp.einsum(
        "nk,nl->kl",
        left_side.reshape(-1, columns_n),
        right_side.reshape(-1, columns_n),
        precision=HIGHEST,
        preferred_element_type=jnp.float32,
    )


def mix_right(vectors, matrix):
    columns_n = vectors.shape[-1]
    return jnp.dot(
        vectors.reshape(-1, columns_n),
        matrix,
        precision=HIGHEST,
        preferred_element_type=jnp.float32,
    ).reshape(vectors.shape)


def solve_spd(matrix, target):
    factor = jnp.linalg.cholesky(matrix)
    return jax.scipy.linalg.cho_solve((factor, True), target)


def to_rowset(column_set, row_index, col_index):
    low_bits = lax.axis_size("row").bit_length() - 1
    high_bits = lax.axis_size("col").bit_length() - 1
    current = column_set
    for bit_pos in range(low_bits):
        partner = partner_2(current, "col", bit_pos)
        differs = col_index >> bit_pos & 1 != row_index >> bit_pos & 1
        current = jnp.where(differs, partner, current)
    joined = current[:, None]
    for bit_pos in range(low_bits, high_bits):
        partner = partner_2(joined, "col", bit_pos)
        lower_half = col_index >> bit_pos & 1 == 0
        joined = jnp.where(
            lower_half,
            jnp.concatenate([joined, partner], axis=1),
            jnp.concatenate([partner, joined], axis=1),
        )
    return joined.reshape((-1,) + column_set.shape[1:])


def to_colset(row_set, col_index):
    rows_n = lax.axis_size("row")
    groups = lax.axis_size("col") // rows_n
    shape_in = row_set.shape
    regrouped = row_set.reshape(shape_in[:-3] + (shape_in[-3] // groups, groups) + shape_in[-2:])
    selected = lax.dynamic_index_in_dim(
        regrouped, col_index // rows_n, regrouped.ndim - 3, keepdims=False
    )
    return spread(selected, "row", col_index % rows_n)


def local_products(lower_part, column_set, row_set):
    columns_n = column_set.shape[-1]
    by_rows = jnp.dot(
        lower_part,
        column_set.reshape(-1, columns_n),
        precision=HIGHEST,
        preferred_element_type=jnp.float32,
    )
    by_columns = jnp.einsum(
        "nm,nk->mk",
        lower_part,
        row_set.reshape(-1, columns_n),
        precision=HIGHEST,
        preferred_element_type=jnp.float32,
    )
    return (by_rows, by_columns)


def columns_whole(by_columns, shape_out):
    return lax.psum(by_columns, "row").reshape(shape_out)


def rows_whole(by_rows, shape_out):
    return lax.psum(by_rows, "col").reshape(shape_out)


def per_device(stored, rhs):
    row_index = lax.axis_index("row")
    col_index = lax.axis_index("col")
    rows_n = lax.axis_size("row")
    cols_n = lax.axis_size("col")
    row_blocks = stored.shape[0]
    block_size = stored.shape[2]
    col_blocks = stored.shape[3]
    columns_n = rhs.shape[-1]
    block_rows = jnp.arange(row_blocks, dtype=jnp.int32) * rows_n + row_index
    block_cols = jnp.arange(col_blocks, dtype=jnp.int32) * cols_n + col_index
    weight = jnp.where(
        block_rows[:, None] > block_cols[None, :],
        1.0,
        jnp.where(block_rows[:, None] == block_cols[None, :], 0.5, 0.0),
    ).astype(jnp.float32)
    lower_part = (
        stored.reshape(row_blocks, block_size, col_blocks, block_size) * weight[:, None, :, None]
    ).reshape(row_blocks * block_size, col_blocks * block_size)
    start_set = rhs.reshape(col_blocks, block_size, columns_n)

    def reduce_grams(stacked):
        return lax.psum(stacked, "row")

    vectors = to_rowset(start_set, row_index, col_index)
    solution = jnp.zeros_like(vectors)
    residual = vectors
    direction = vectors
    gram_now = reduce_grams(gram_local(residual, residual)[None])[0]
    for iteration in range(ITERS):
        column_set = to_colset(direction, col_index)
        by_rows, by_columns = local_products(lower_part, column_set, direction)
        row_part = rows_whole(by_rows, direction.shape)
        applied = row_part + to_rowset(
            columns_whole(by_columns, column_set.shape), row_index, col_index
        )
        last_turn = iteration + 1 == ITERS
        gram_sums = reduce_grams(gram_local(direction, applied)[None])
        curvature = gram_sums[0]
        step_size = solve_spd(curvature, gram_now)
        solution = solution + mix_right(direction, step_size)
        residual = residual - mix_right(applied, step_size)
        if not last_turn:
            gram_next = reduce_grams(gram_local(residual, residual)[None])[0]
            mix_factor = solve_spd(gram_now, gram_next)
            direction = residual + mix_right(direction, mix_factor)
            gram_now = gram_next
    both_sets = to_colset(jnp.stack([solution, residual]), col_index)
    final_pair = (both_sets[0], both_sets[1])
    return (final_pair[0].reshape(rhs.shape), final_pair[1].reshape(rhs.shape))


def solution(mesh):
    placed = (P(None, "row", None, None, "col", None), P(None, "col", None, None))
    return jax.shard_map(
        per_device,
        mesh=mesh,
        in_specs=placed,
        out_specs=(P(None, "col", None, None), P(None, "col", None, None)),
        check_vma=False,
    )
```

profile of v0, /device:TPU:2, one launch (start us, length us, event | category | flops | bytes accessed | tf_op | source)
XLA Modules:
  0.0 995.7 jit_solution(8550308270842308896)
XLA Ops:
  9.2 7.9 collective-permute-done
  21.5 14.1 %collective-permute-done.1 = f32[5,128,128]{2,1,0:T(8,128)S(1)} collective-permute-done((f32[5,128,128]{2,1,0:T(8,128)S(1)}, f32[5,128,128]{2,1,0:T(8,128)S(1)}, u32[]{:S(2)}, u32[]{:S(2)}) %collective-permute-start.1) | collective-permute-done | bytes 327712 | tf_op jit(solution)/shard_map/ppermute | solution.py:13
  35.6 6.3 collective-permute-start.2
  41.9 14.5 %collective-permute-done.2 = f32[5,128,128]{2,1,0:T(8,128)S(1)} collective-permute-done((f32[5,128,128]{2,1,0:T(8,128)S(1)}, f32[5,128,128]{2,1,0:T(8,128)S(1)}, u32[]{:S(2)}, u32[]{:S(2)}) %collective-permute-start.2) | collective-permute-done | bytes 327712 | tf_op jit(solution)/shard_map/ppermute | solution.py:13
  57.1 6.7 collective-permute-done.3
  67.2 23.9 %multiply_reduce_fusion = f32[20,128,5,128]{3,2,1,0:T(8,128)} fusion(f32[20,1,128,5,1,128]{5,4,3,2,1,0:T(1,128)} %param.5, f32[20,5]{1,0:T(8,128)S(1)} %select_select_fusion.3), kind=kLoop, calls=%fused_computation.8 | loop fusion | flops 1638400 | bytes 13107600 | tf_op jit(solution)/shard_map/mul | solution.py:121
  91.9 14.6 %fusion.4 = f32[640,128]{1,0:T(8,128)} fusion(f32[2560,128]{1,0:T(8,128)S(1)} %bitcast.127, f32[320,8,5,128]{3,2,1,0:T(8,128)} %bitcast.123), kind=kOutput, calls=%fused_computation.4 | convolution fusion | flops 2516582400 | bytes 8192000 | tf_op jit(solution)/shard_map/nm,nk->mk/dot_general | solution.py:86
  106.6 65.4 %all-reduce.26.cloned.1.call-done = (f32[640,128]{1,0:T(8,128)}, f32[5,128,128]{2,1,0:T(8,128)}) async-done(((f32[640,128]{1,0:T(8,128)}, f32[5,128,128]{2,1,0:T(8,128)}), (f32[640,128]{1,0:T(8,128)}, f32[5,128,128]{2,1,0:T(8,128)})) %all-reduce.26.cloned.1.call-update) | async-done | bytes 655376 | tf_op jit(solution)/shard_map/psum | solution.py:18
  173.5 6.1 collective-permute-done.5
  183.5 10.9 %collective-permute-done.6 = f32[5,128,128]{2,1,0:T(8,128)S(1)} collective-permute-done((f32[5,128,128]{2,1,0:T(8,128)S(1)}, f32[5,128,128]{2,1,0:T(8,128)S(1)}, u32[]{:S(2)}, u32[]{:S(2)}) %collective-permute-start.6) | collective-permute-done | bytes 327712 | tf_op jit(solution)/shard_map/ppermute | solution.py:13
  200.2 10.1 %fusion.6 = f32[2560,128]{1,0:T(8,128)} fusion(f32[640,128]{1,0:T(8,128)S(1)} %copy-done.5, f32[320,8,5,128]{3,2,1,0:T(8,128)} %bitcast.124), kind=kOutput, calls=%fused_computation.6 | convolution fusion | flops 2516582400 | bytes 8192000 | tf_op jit(solution)/shard_map/dot_general | solution.py:80
  214.8 6.5 collective-permute-done.8
  228.5 11.5 %collective-permute-done.9 = f32[5,2,128,128]{3,2,0,1:T(8,128)S(1)} collective-permute-done((f32[5,2,128,128]{3,2,0,1:T(8,128)S(1)}, f32[5,2,128,128]{3,2,0,1:T(8,128)S(1)}, u32[]{:S(2)}, u32[]{:S(2)}) %collective-permute-start.9) | collective-permute-done | bytes 655392 | tf_op jit(solution)/shard_map/ppermute | solution.py:13
  241.3 126.0 %all-reduce.12.cloned.1.call-done = f32[2560,128]{1,0:T(8,128)} async-done(((f32[2560,128]{1,0:T(8,128)}), f32[2560,128]{1,0:T(8,128)}) %all-reduce.12.cloned.1.call-update) | async-done | bytes 1310736 | tf_op jit(solution)/shard_map/psum | solution.py:101
  372.4 62.7 %all-reduce.24.cloned.1.call-done = (f32[128,128]{0,1:T(8,128)}, f32[128,128]{0,1:T(8,128)}) async-done(((f32[128,128]{0,1:T(8,128)}, f32[128,128]{0,1:T(8,128)}), (f32[128,128]{0,1:T(8,128)}, f32[128,128]{0,1:T(8,128)})) %all-reduce.24.cloned.1.call-update) | async-done | bytes 131088 | tf_op jit(solution)/shard_map/psum | solution.py:126
  438.0 11.7 %cholesky.70 = f32[128,128]{1,0:T(8,128)S(1)} custom-call(f32[128,128]{1,0:T(8,128)S(1)} %get-tuple-element.12), custom_call_target="Cholesky" | custom-call | tf_op jit(solution)/shard_map/jit(cholesky)/cholesky | solution.py:43
  450.3 11.7 %cholesky.59 = f32[128,128]{1,0:T(8,128)S(1)} custom-call(f32[128,128]{1,0:T(8,128)S(1)} %get-tuple-element.13), custom_call_target="Cholesky" | custom-call | tf_op jit(solution)/shard_map/jit(cholesky)/cholesky | solution.py:43
  463.4 9.8 custom-call.9
  480.8 9.8 custom-call.10
  490.6 52.6 %all-reduce.14.cloned.1.call-done = f32[128,128]{1,0:T(8,128)} async-done(((f32[128,128]{1,0:T(8,128)}), f32[128,128]{1,0:T(8,128)}) %all-reduce.14.cloned.1.call-update) | async-done | bytes 65552 | tf_op jit(solution)/shard_map/psum | solution.py:126
  546.6 14.6 %fusion = f32[640,128]{1,0:T(8,128)} fusion(f32[2560,128]{1,0:T(8,128)S(1)} %bitcast.133, f32[320,8,5,128]{3,2,1,0:T(8,128)} %bitcast.125), kind=kOutput, calls=%fused_computation | convolution fusion | flops 2516582400 | bytes 8192000 | tf_op jit(solution)/shard_map/nm,nk->mk/dot_general | solution.py:86
  561.3 65.7 %all-reduce.22.cloned.1.call-done = (f32[640,128]{1,0:T(8,128)}, f32[5,128,128]{2,1,0:T(8,128)}) async-done(((f32[640,128]{1,0:T(8,128)}, f32[5,128,128]{2,1,0:T(8,128)}), (f32[640,128]{1,0:T(8,128)}, f32[5,128,128]{2,1,0:T(8,128)})) %all-reduce.22.cloned.1.call-update) | async-done | bytes 655376 | tf_op jit(solution)/shard_map/psum | solution.py:18
  628.5 6.1 collective-permute-done.10
  638.5 10.9 %collective-permute-done.11 = f32[5,128,128]{2,1,0:T(8,128)S(1)} collective-permute-done((f32[5,128,128]{2,1,0:T(8,128)S(1)}, f32[5,128,128]{2,1,0:T(8,128)S(1)}, u32[]{:S(2)}, u32[]{:S(2)}) %collective-permute-start.11) | collective-permute-done | bytes 327712 | tf_op jit(solution)/shard_map/ppermute | solution.py:13
  655.2 10.1 %fusion.2 = f32[2560,128]{1,0:T(8,128)} fusion(f32[640,128]{1,0:T(8,128)S(1)} %copy-done.4, f32[320,8,5,128]{3,2,1,0:T(8,128)} %bitcast.126), kind=kOutput, calls=%fused_computation.2 | convolution fusion | flops 2516582400 | bytes 8192000 | tf_op jit(solution)/shard_map/dot_general | solution.py:80
  669.8 6.5 collective-permute-done.13
  680.6 14.4 %collective-permute-done.14 = f32[5,2,128,128]{3,2,0,1:T(8,128)S(1)} collective-permute-done((f32[5,2,128,128]{3,2,0,1:T(8,128)S(1)}, f32[5,2,128,128]{3,2,0,1:T(8,128)S(1)}, u32[]{:S(2)}, u32[]{:S(2)}) %collective-permute-start.14) | collective-permute-done | bytes 655392 | tf_op jit(solution)/shard_map/ppermute | solution.py:13
  696.3 126.0 %all-reduce.16.cloned.1.call-done = f32[2560,128]{1,0:T(8,128)} async-done(((f32[2560,128]{1,0:T(8,128)}), f32[2560,128]{1,0:T(8,128)}) %all-reduce.16.cloned.1.call-update) | async-done | bytes 1310736 | tf_op jit(solution)/shard_map/psum | solution.py:101
  830.5 59.3 %all-reduce.18.cloned.1.call-done = f32[128,128]{0,1:T(8,128)} async-done(((f32[128,128]{0,1:T(8,128)}), f32[128,128]{0,1:T(8,128)}) %all-reduce.18.cloned.1.call-update) | async-done | bytes 65552 | tf_op jit(solution)/shard_map/psum | solution.py:126
  891.6 11.7 %cholesky.81 = f32[128,128]{1,0:T(8,128)S(1)} custom-call(f32[128,128]{1,0:T(8,128)S(1)} %fusion.18), custom_call_target="Cholesky" | custom-call | tf_op jit(solution)/shard_map/jit(cholesky)/cholesky | solution.py:43
  904.7 9.8 custom-call.11
  920.9 65.6 %all-reduce.20.cloned.1.call-done = f32[2,5,128,128]{3,2,1,0:T(8,128)} async-done(((f32[2,5,128,128]{3,2,1,0:T(8,128)}), f32[2,5,128,128]{3,2,1,0:T(8,128)}) %all-reduce.20.cloned.1.call-update) | async-done | bytes 655376 | tf_op jit(solution)/shard_map/psum | solution.py:18
  (103 shorter events, 97.3 us)
Async XLA Ops:
  7.2 164.8 %all-reduce.26.cloned.1.call-start = ((), (), s32[]{:S(2)}) async-start(), calls=%async_computation.7 | async-start | bytes 1310720 | tf_op jit(solution)/shard_map/psum | solution.py:18
  7.2 9.9 collective-permute-start
  18.1 17.4 %collective-permute-start.1 = (f32[5,128,128]{2,1,0:T(8,128)S(1)}, f32[5,128,128]{2,1,0:T(8,128)S(1)}, u32[]{:S(2)}, u32[]{:S(2)}) collective-permute-start(f32[5,128,128]{2,1,0:T(8,128)S(1)} %broadcast_select_fusion.2), channel_id=1, source_target_pairs={{0,2},{1,3},{2,0},{3,1},{4,6},{5,7},{6,4},{7,5},{8,10},{9,11},{10,... | collective-permute-start | bytes 983048 | tf_op jit(solution)/shard_map/ppermute | solution.py:13
  35.6 20.8 %collective-permute-start.2 = (f32[5,128,128]{2,1,0:T(8,128)S(1)}, f32[5,128,128]{2,1,0:T(8,128)S(1)}, u32[]{:S(2)}, u32[]{:S(2)}) collective-permute-start(f32[5,128,128]{2,1,0:T(8,128)S(1)} %broadcast_select_fusion.5), channel_id=1, source_target_pairs={{0,4},{1,5},{2,6},{3,7},{4,0},{5,1},{6,2},{7,3},{8,12},{9,13},{10,... | collective-permute-start | bytes 983048 | tf_op jit(solution)/shard_map/ppermute | solution.py:13
  56.4 7.4 collective-permute-start.3
  63.9 27.2 %collective-permute-start.4 = (f32[5,2,128,128]{3,2,1,0:T(8,128)S(1)}, f32[5,2,128,128]{3,2,1,0:T(8,128)S(1)}, u32[]{:S(2)}, u32[]{:S(2)}) collective-permute-start(f32[5,2,128,128]{3,2,1,0:T(8,128)S(1)} %maximum_select_fusion.3), channel_id=1, source_target_pairs={{0,16},{1,17},{2,18},{3,19},{4,20},{5,21},{6,22},{7,23},{8,24},{9,... | collective-permute-start | bytes 1966088 | tf_op jit(solution)/shard_map/ppermute | solution.py:13
  106.5 260.7 %all-reduce.12.cloned.1.call-start = ((), (), s32[]{:S(2)}) async-start(), calls=%async_computation | async-start | bytes 2621440 | tf_op jit(solution)/shard_map/psum | solution.py:101
  171.9 28.3 %copy-start.5 = (f32[640,128]{1,0:T(8,128)S(1)}, f32[640,128]{1,0:T(8,128)}, u32[]{:S(2)}) copy-start(f32[640,128]{1,0:T(8,128)} %get-tuple-element.8) | copy-start | bytes 983044
  171.9 7.6 collective-permute-start.5
  180.6 13.8 %collective-permute-start.6 = (f32[5,128,128]{2,1,0:T(8,128)S(1)}, f32[5,128,128]{2,1,0:T(8,128)S(1)}, u32[]{:S(2)}, u32[]{:S(2)}) collective-permute-start(f32[5,128,128]{2,1,0:T(8,128)S(1)} %broadcast_select_fusion.1), channel_id=1, source_target_pairs={{0,2},{1,3},{2,0},{3,1},{4,6},{5,7},{6,4},{7,5},{8,10},{9,11},{10,... | collective-permute-start | bytes 983048 | tf_op jit(solution)/shard_map/ppermute | solution.py:13
  194.4 19.7 %collective-permute-start.7 = (f32[5,128,128]{2,1,0:T(8,128)S(1)}, f32[5,128,128]{2,1,0:T(8,128)S(1)}, u32[]{:S(2)}, u32[]{:S(2)}) collective-permute-start(f32[5,128,128]{2,1,0:T(8,128)S(1)} %broadcast_select_fusion.4), channel_id=1, source_target_pairs={{0,4},{1,5},{2,6},{3,7},{4,0},{5,1},{6,2},{7,3},{8,12},{9,13},{10,... | collective-permute-start | bytes 983048 | tf_op jit(solution)/shard_map/ppermute | solution.py:13
  210.4 224.8 %all-reduce.24.cloned.1.call-start = ((), (), s32[]{:S(2)}) async-start(), calls=%async_computation.6 | async-start | bytes 262144 | tf_op jit(solution)/shard_map/psum | solution.py:126
  214.2 7.2 collective-permute-start.8
  221.4 18.6 %collective-permute-start.9 = (f32[5,2,128,128]{3,2,0,1:T(8,128)S(1)}, f32[5,2,128,128]{3,2,0,1:T(8,128)S(1)}, u32[]{:S(2)}, u32[]{:S(2)}) collective-permute-start(f32[5,2,128,128]{3,2,0,1:T(8,128)S(1)} %maximum_select_fusion.4), channel_id=1, source_target_pairs={{0,16},{1,17},{2,18},{3,19},{4,20},{5,21},{6,22},{7,23},{8,24},{9,... | collective-permute-start | bytes 1966088 | tf_op jit(solution)/shard_map/ppermute | solution.py:13
  369.1 2.9 copy-start.2
  372.0 171.2 %all-reduce.14.cloned.1.call-start = ((), (), s32[]{:S(2)}) async-start(), calls=%async_computation.1 | async-start | bytes 131072 | tf_op jit(solution)/shard_map/psum | solution.py:126
  480.1 146.9 %all-reduce.22.cloned.1.call-start = ((), (), s32[]{:S(2)}) async-start(), calls=%async_computation.5 | async-start | bytes 1310720 | tf_op jit(solution)/shard_map/psum | solution.py:18
  545.8 15.4 %copy-start = (f32[20,128,128]{2,1,0:T(8,128)}, f32[20,128,128]{2,1,0:T(8,128)S(1)}, u32[]{:S(2)}) copy-start(f32[20,128,128]{2,1,0:T(8,128)S(1)} %convolution_add_fusion) | copy-start | bytes 3932164
  561.2 261.0 %all-reduce.16.cloned.1.call-start = ((), (), s32[]{:S(2)}) async-start(), calls=%async_computation.2 | async-start | bytes 2621440 | tf_op jit(solution)/shard_map/psum | solution.py:101
  627.0 28.3 %copy-start.4 = (f32[640,128]{1,0:T(8,128)S(1)}, f32[640,128]{1,0:T(8,128)}, u32[]{:S(2)}) copy-start(f32[640,128]{1,0:T(8,128)} %get-tuple-element.4) | copy-start | bytes 983044
  627.0 7.6 collective-permute-start.10
  635.6 13.8 %collective-permute-start.11 = (f32[5,128,128]{2,1,0:T(8,128)S(1)}, f32[5,128,128]{2,1,0:T(8,128)S(1)}, u32[]{:S(2)}, u32[]{:S(2)}) collective-permute-start(f32[5,128,128]{2,1,0:T(8,128)S(1)} %broadcast_select_fusion), channel_id=1, source_target_pairs={{0,2},{1,3},{2,0},{3,1},{4,6},{5,7},{6,4},{7,5},{8,10},{9,11},{10,... | collective-permute-start | bytes 983048 | tf_op jit(solution)/shard_map/ppermute | solution.py:13
  649.4 19.7 %collective-permute-start.12 = (f32[5,128,128]{2,1,0:T(8,128)S(1)}, f32[5,128,128]{2,1,0:T(8,128)S(1)}, u32[]{:S(2)}, u32[]{:S(2)}) collective-permute-start(f32[5,128,128]{2,1,0:T(8,128)S(1)} %broadcast_select_fusion.3), channel_id=1, source_target_pairs={{0,4},{1,5},{2,6},{3,7},{4,0},{5,1},{6,2},{7,3},{8,12},{9,13},{10,... | collective-permute-start | bytes 983048 | tf_op jit(solution)/shard_map/ppermute | solution.py:13
  665.4 224.4 %all-reduce.18.cloned.1.call-start = ((), (), s32[]{:S(2)}) async-start(), calls=%async_computation.3 | async-start | bytes 131072 | tf_op jit(solution)/shard_map/psum | solution.py:126
  669.2 7.2 collective-permute-start.13
  676.4 18.6 %collective-permute-start.14 = (f32[5,2,128,128]{3,2,0,1:T(8,128)S(1)}, f32[5,2,128,128]{3,2,0,1:T(8,128)S(1)}, u32[]{:S(2)}, u32[]{:S(2)}) collective-permute-start(f32[5,2,128,128]{3,2,0,1:T(8,128)S(1)} %maximum_select_fusion.5), channel_id=1, source_target_pairs={{0,16},{1,17},{2,18},{3,19},{4,20},{5,21},{6,22},{7,23},{8,24},{9,... | collective-permute-start | bytes 1966088 | tf_op jit(solution)/shard_map/ppermute | solution.py:13
  822.2 2.1 copy-start.1
  827.3 87.2 %copy-start.6 = (f32[128,128]{1,0:T(8,128)S(1)}, f32[128,128]{1,0:T(8,128)}, u32[]{:S(2)}) copy-start(f32[128,128]{1,0:T(8,128)} %all-reduce.14.cloned.1.call-done) | copy-start | bytes 196612
  827.3 159.2 %all-reduce.20.cloned.1.call-start = ((), (), s32[]{:S(2)}) async-start(), calls=%async_computation.4 | async-start | bytes 1310720 | tf_op jit(solution)/shard_map/psum | solution.py:18
  915.0 2.6 copy-start.3
Sparse Core Ops, SparseCore 0:
  106.6 65.2 all-reduce.25
  210.5 156.6 all-reduce.11
  372.1 63.0 all-reduce.23
  480.2 62.9 all-reduce.13
  561.3 65.5 all-reduce.21
  665.5 156.6 all-reduce.15
  827.4 62.3 all-reduce.17
  921.0 65.3 all-reduce.19
where the time goes:
time: 1000 us; the launch traced here: 996 us
  waiting for transfers between devices  747 us (75%)
  other arithmetic  107 us (11%)
  matrix products  72.8 us (7%)
  starting transfers between devices  46.7 us (5%)
  between operations  14.9 us (1%)
    psum x2, waiting for transfers between devices, rows_whole(): return lax.psum(by_rows, 'col').reshape(shape_out)  252 us
    psum x3, waiting for transfers between devices, spread(): return lax.psum(kept, axis)  197 us
    psum x3, waiting for transfers between devices, reduce_grams(): return lax.psum(stacked, 'row')  175 us
    ppermute x15, waiting for transfers between devices, partner_2(): return lax.ppermute(value, axis, pairs)  124 us
    ppermute x15, starting transfers between devices, partner_2(): return lax.ppermute(value, axis, pairs)  45.8 us
    another operation x9, other arithmetic, solve_spd(): factor = jnp.linalg.cholesky(matrix)  37.2 us
    another operation x6, other arithmetic, solve_spd(): return jax.scipy.linalg.cho_solve((factor, True), target)  31.4 us
    dot_general x2, matrix products, local_products(): jnp.einsum('nm,nk->mk', lower_part, row_set.reshape(-1, columns_n), preci...  29.2 us
  transfers between devices with their start and end apart: 23, of which 22 were waited for; matrix products, arithmetic and copies ran while one was open for 6% of the time, Pallas kernels for 0%

commit v1 on v0

--- a/solution.py
+++ b/solution.py
@@ -123,7 +123,11 @@
     start_set = rhs.reshape(col_blocks, block_size, columns_n)
 
     def reduce_grams(stacked):
-        return lax.psum(stacked, "row")
+
+        def feed_rounds(body, ax_name):
+            return lax.all_gather(body, ax_name).sum(axis=0)
+
+        return feed_rounds(stacked, "row")
 
     vectors = to_rowset(start_set, row_index, col_index)
     solution = jnp.zeros_like(vectors)

time: 1000 us -> 838 us (0.84)
  waiting for transfers between devices: 747 us -> 538 us
  blocking collectives: 0 us -> 57.4 us
    psum x3 -> x0, waiting for transfers between devices: 175 us -> none  [reduce_grams(): return lax.psum(stacked, 'row')]
    all_gather x0 -> x4, blocking collectives: none -> 57.4 us  [feed_rounds(): return lax.all_gather(body, ax_name).sum(axis=0)]
    ppermute x15, waiting for transfers between devices: 124 us -> 105 us  [partner_2(): return lax.ppermute(value, axis, pairs)]
    psum x2, waiting for transfers between devices: 252 us -> 238 us  [rows_whole(): return lax.psum(by_rows, 'col').reshape(shape_out)]
  transfers between devices with their start and end apart: 23 -> 20, of which waited for: 22 -> 17; matrix products, arithmetic and copies ran while one was open for 6% -> 9% of each run, Pallas kernels for 0% -> 0%
where the time goes in v1:
time: 838 us; the launch traced here: 829 us
  waiting for transfers between devices  538 us (64%)
  other arithmetic  102 us (12%)
  matrix products  68.5 us (8%)
  blocking collectives  57.4 us (7%)
  starting transfers between devices  44.9 us (5%)
  between operations  14.4 us (2%)
    psum x2, waiting for transfers between devices, rows_whole(): return lax.psum(by_rows, 'col').reshape(shape_out)  238 us
    psum x3, waiting for transfers between devices, spread(): return lax.psum(kept, axis)  194 us
    ppermute x15, waiting for transfers between devices, partner_2(): return lax.ppermute(value, axis, pairs)  105 us
    all_gather x4, blocking collectives, feed_rounds(): return lax.all_gather(body, ax_name).sum(axis=0)  57.4 us
    ppermute x15, starting transfers between devices, partner_2(): return lax.ppermute(value, axis, pairs)  44.7 us
    another operation x9, other arithmetic, solve_spd(): factor = jnp.linalg.cholesky(matrix)  37.2 us
    another operation x6, other arithmetic, solve_spd(): return jax.scipy.linalg.cho_solve((factor, True), target)  31.4 us
    dot_general x2, matrix products, local_products(): jnp.einsum('nm,nk->mk', lower_part, row_set.reshape(-1, columns_n), preci...  29.2 us
  transfers between devices with their start and end apart: 20, of which 17 were waited for; matrix products, arithmetic and copies ran while one was open for 9% of the time, Pallas kernels for 0%

profile of v1, /device:TPU:2, one launch (start us, length us, event | category | flops | bytes accessed | tf_op | source)
XLA Modules:
  0.0 829.0 jit_solution(2438360447609790277)
XLA Ops:
  9.2 7.9 collective-permute-done
  21.5 14.1 %collective-permute-done.1 = f32[5,128,128]{2,1,0:T(8,128)S(1)} collective-permute-done((f32[5,128,128]{2,1,0:T(8,128)S(1)}, f32[5,128,128]{2,1,0:T(8,128)S(1)}, u32[]{:S(2)}, u32[]{:S(2)}) %collective-permute-start.1) | collective-permute-done | bytes 327712 | tf_op jit(solution)/shard_map/ppermute | solution.py:13
  35.6 6.3 collective-permute-start.2
  41.9 14.5 %collective-permute-done.2 = f32[5,128,128]{2,1,0:T(8,128)S(1)} collective-permute-done((f32[5,128,128]{2,1,0:T(8,128)S(1)}, f32[5,128,128]{2,1,0:T(8,128)S(1)}, u32[]{:S(2)}, u32[]{:S(2)}) %collective-permute-start.2) | collective-permute-done | bytes 327712 | tf_op jit(solution)/shard_map/ppermute | solution.py:13
  57.1 6.7 collective-permute-done.3
  67.2 23.9 %multiply_reduce_fusion = f32[20,128,5,128]{3,2,1,0:T(8,128)} fusion(f32[20,1,128,5,1,128]{5,4,3,2,1,0:T(1,128)} %param.5, f32[20,5]{1,0:T(8,128)S(1)} %select_select_fusion.3), kind=kLoop, calls=%fused_computation.8 | loop fusion | flops 1638400 | bytes 13107600 | tf_op jit(solution)/shard_map/mul | solution.py:121
  91.9 14.6 %fusion.4 = f32[640,128]{1,0:T(8,128)} fusion(f32[2560,128]{1,0:T(8,128)S(1)} %bitcast.133, f32[320,8,5,128]{3,2,1,0:T(8,128)} %bitcast.129), kind=kOutput, calls=%fused_computation.4 | convolution fusion | flops 2516582400 | bytes 8192000 | tf_op jit(solution)/shard_map/nm,nk->mk/dot_general | solution.py:86
  106.6 65.4 %all-reduce.16.cloned.1.call-done = (f32[640,128]{1,0:T(8,128)}, f32[5,128,128]{2,1,0:T(8,128)}) async-done(((f32[640,128]{1,0:T(8,128)}, f32[5,128,128]{2,1,0:T(8,128)}), (f32[640,128]{1,0:T(8,128)}, f32[5,128,128]{2,1,0:T(8,128)})) %all-reduce.16.cloned.1.call-update) | async-done | bytes 655376 | tf_op jit(solution)/shard_map/psum | solution.py:18
  173.5 6.1 collective-permute-done.5
  183.7 10.9 %collective-permute-done.6 = f32[5,128,128]{2,1,0:T(8,128)S(1)} collective-permute-done((f32[5,128,128]{2,1,0:T(8,128)S(1)}, f32[5,128,128]{2,1,0:T(8,128)S(1)}, u32[]{:S(2)}, u32[]{:S(2)}) %collective-permute-start.6) | collective-permute-done | bytes 327712 | tf_op jit(solution)/shard_map/ppermute | solution.py:13
  200.5 10.1 %fusion.6 = f32[2560,128]{1,0:T(8,128)} fusion(f32[640,128]{1,0:T(8,128)S(1)} %copy-done.6, f32[320,8,5,128]{3,2,1,0:T(8,128)} %bitcast.130), kind=kOutput, calls=%fused_computation.6 | convolution fusion | flops 2516582400 | bytes 8192000 | tf_op jit(solution)/shard_map/dot_general | solution.py:80
  217.3 16.8 %all-gather.1 = f32[1024,128]{1,0:T(8,128)S(1)} all-gather(f32[128,128]{1,0:T(8,128)S(1)} %convolution_bitcast_fusion.5), channel_id=3, replica_groups=mesh['row'=8,'col'=32] {'row'}, dimensions={0}, use_global_device_ids=true | all-gather | bytes 589824 | tf_op jit(solution)/shard_map/all_gather | solution.py:128
  236.9 11.7 %cholesky.70 = f32[128,128]{1,0:T(8,128)S(1)} custom-call(f32[128,128]{1,0:T(8,128)S(1)} %fusion.22), custom_call_target="Cholesky" | custom-call | tf_op jit(solution)/shard_map/jit(cholesky)/cholesky | solution.py:43
  250.0 9.8 %custom-call.10 = f32[1,128,128]{1,2,0:T(8,128)S(1)} custom-call(f32[1,128,128]{2,1,0:T(8,128)S(1)} %fusion.13), custom_call_target="InvertDiagBlocksLowerTriangular" | custom-call | tf_op jit(solution)/shard_map/jit(_cho_solve)/triangular_solve | solution.py:44
  260.0 110.8 %all-reduce.8.cloned.1.call-done = f32[2560,128]{1,0:T(8,128)} async-done(((f32[2560,128]{1,0:T(8,128)}), f32[2560,128]{1,0:T(8,128)}) %all-reduce.8.cloned.1.call-update) | async-done | bytes 1310736 | tf_op jit(solution)/shard_map/psum | solution.py:101
  374.5 13.7 %all-gather = f32[1024,128]{1,0:T(8,128)S(1)} all-gather(f32[128,128]{1,0:T(8,128)S(1)} %fusion.31), channel_id=2, replica_groups=mesh['row'=8,'col'=32] {'row'}, dimensions={0}, use_global_device_ids=true | all-gather | bytes 589824 | tf_op jit(solution)/shard_map/all_gather | solution.py:128
  388.3 11.7 %cholesky.59 = f32[128,128]{1,0:T(8,128)S(1)} custom-call(f32[128,128]{1,0:T(8,128)S(1)} %fusion.26), custom_call_target="Cholesky" | custom-call | tf_op jit(solution)/shard_map/jit(cholesky)/cholesky | solution.py:43
  401.4 9.8 %custom-call.9 = f32[1,128,128]{1,2,0:T(8,128)S(1)} custom-call(f32[1,128,128]{2,1,0:T(8,128)S(1)} %fusion.12), custom_call_target="InvertDiagBlocksLowerTriangular" | custom-call | tf_op jit(solution)/shard_map/jit(_cho_solve)/triangular_solve | solution.py:44
  416.4 13.4 %all-gather.2 = f32[1024,128]{1,0:T(8,128)S(1)} all-gather(f32[128,128]{1,0:T(8,128)S(1)} %convolution_bitcast_fusion.4), channel_id=4, replica_groups=mesh['row'=8,'col'=32] {'row'}, dimensions={0}, use_global_device_ids=true | all-gather | bytes 589824 | tf_op jit(solution)/shard_map/all_gather | solution.py:128
  432.4 14.6 %fusion = f32[640,128]{1,0:T(8,128)} fusion(f32[2560,128]{1,0:T(8,128)S(1)} %bitcast.139, f32[320,8,5,128]{3,2,1,0:T(8,128)} %bitcast.131), kind=kOutput, calls=%fused_computation | convolution fusion | flops 2516582400 | bytes 8192000 | tf_op jit(solution)/shard_map/nm,nk->mk/dot_general | solution.py:86
  447.0 64.5 %all-reduce.14.cloned.1.call-done = (f32[640,128]{1,0:T(8,128)}, f32[5,128,128]{2,1,0:T(8,128)}) async-done(((f32[640,128]{1,0:T(8,128)}, f32[5,128,128]{2,1,0:T(8,128)}), (f32[640,128]{1,0:T(8,128)}, f32[5,128,128]{2,1,0:T(8,128)})) %all-reduce.14.cloned.1.call-update) | async-done | bytes 655376 | tf_op jit(solution)/shard_map/psum | solution.py:18
  513.1 6.1 collective-permute-done.10
  522.8 10.9 %collective-permute-done.11 = f32[5,128,128]{2,1,0:T(8,128)S(1)} collective-permute-done((f32[5,128,128]{2,1,0:T(8,128)S(1)}, f32[5,128,128]{2,1,0:T(8,128)S(1)}, u32[]{:S(2)}, u32[]{:S(2)}) %collective-permute-start.11) | collective-permute-done | bytes 327712 | tf_op jit(solution)/shard_map/ppermute | solution.py:13
  533.8 6.3 collective-permute-start.12
  540.1 10.1 %fusion.2 = f32[2560,128]{1,0:T(8,128)} fusion(f32[640,128]{1,0:T(8,128)S(1)} %copy-done.5, f32[320,8,5,128]{3,2,1,0:T(8,128)} %bitcast.132), kind=kOutput, calls=%fused_computation.2 | convolution fusion | flops 2516582400 | bytes 8192000 | tf_op jit(solution)/shard_map/dot_general | solution.py:80
  554.8 6.5 collective-permute-done.13
  565.6 14.3 %collective-permute-done.14 = f32[5,2,128,128]{3,2,0,1:T(8,128)S(1)} collective-permute-done((f32[5,2,128,128]{3,2,0,1:T(8,128)S(1)}, f32[5,2,128,128]{3,2,0,1:T(8,128)S(1)}, u32[]{:S(2)}, u32[]{:S(2)}) %collective-permute-start.14) | collective-permute-done | bytes 655392 | tf_op jit(solution)/shard_map/ppermute | solution.py:13
  581.2 126.9 %all-reduce.10.cloned.1.call-done = f32[2560,128]{1,0:T(8,128)} async-done(((f32[2560,128]{1,0:T(8,128)}), f32[2560,128]{1,0:T(8,128)}) %all-reduce.10.cloned.1.call-update) | async-done | bytes 1310736 | tf_op jit(solution)/shard_map/psum | solution.py:101
  712.5 13.6 %all-gather.3 = f32[1024,128]{1,0:T(8,128)S(1)} all-gather(f32[128,128]{1,0:T(8,128)S(1)} %convolution_bitcast_fusion.3), channel_id=5, replica_groups=mesh['row'=8,'col'=32] {'row'}, dimensions={0}, use_global_device_ids=true | all-gather | bytes 589824 | tf_op jit(solution)/shard_map/all_gather | solution.py:128
  726.3 11.7 %cholesky.81 = f32[128,128]{1,0:T(8,128)S(1)} custom-call(f32[128,128]{1,0:T(8,128)S(1)} %fusion.18), custom_call_target="Cholesky" | custom-call | tf_op jit(solution)/shard_map/jit(cholesky)/cholesky | solution.py:43
  739.4 9.8 %custom-call.11 = f32[1,128,128]{1,2,0:T(8,128)S(1)} custom-call(f32[1,128,128]{2,1,0:T(8,128)S(1)} %fusion.14), custom_call_target="InvertDiagBlocksLowerTriangular" | custom-call | tf_op jit(solution)/shard_map/jit(_cho_solve)/triangular_solve | solution.py:44
  755.8 64.5 %all-reduce.12.cloned.1.call-done = f32[2,5,128,128]{3,2,1,0:T(8,128)} async-done(((f32[2,5,128,128]{3,2,1,0:T(8,128)}), f32[2,5,128,128]{3,2,1,0:T(8,128)}) %all-reduce.12.cloned.1.call-update) | async-done | bytes 655376 | tf_op jit(solution)/shard_map/psum | solution.py:18
  (103 shorter events, 76.7 us)
Async XLA Ops:
  7.2 164.8 %all-reduce.16.cloned.1.call-start = ((), (), s32[]{:S(2)}) async-start(), calls=%async_computation.4 | async-start | bytes 1310720 | tf_op jit(solution)/shard_map/psum | solution.py:18
  7.2 9.9 %collective-permute-start = (f32[5,128,128]{2,1,0:T(8,128)}, f32[5,128,128]{2,1,0:T(8,128)S(1)}, u32[]{:S(2)}, u32[]{:S(2)}) collective-permute-start(f32[5,128,128]{2,1,0:T(8,128)} %bitcast.153), channel_id=1, source_target_pairs={{0,1},{1,0},{2,3},{3,2},{4,5},{5,4},{6,7},{7,6},{8,9},{9,8},{10,11... | collective-permute-start | bytes 983048 | tf_op jit(solution)/shard_map/ppermute | solution.py:13
  18.1 17.4 %collective-permute-start.1 = (f32[5,128,128]{2,1,0:T(8,128)S(1)}, f32[5,128,128]{2,1,0:T(8,128)S(1)}, u32[]{:S(2)}, u32[]{:S(2)}) collective-permute-start(f32[5,128,128]{2,1,0:T(8,128)S(1)} %broadcast_select_fusion.2), channel_id=1, source_target_pairs={{0,2},{1,3},{2,0},{3,1},{4,6},{5,7},{6,4},{7,5},{8,10},{9,11},{10,... | collective-permute-start | bytes 983048 | tf_op jit(solution)/shard_map/ppermute | solution.py:13
  35.6 20.8 %collective-permute-start.2 = (f32[5,128,128]{2,1,0:T(8,128)S(1)}, f32[5,128,128]{2,1,0:T(8,128)S(1)}, u32[]{:S(2)}, u32[]{:S(2)}) collective-permute-start(f32[5,128,128]{2,1,0:T(8,128)S(1)} %broadcast_select_fusion.5), channel_id=1, source_target_pairs={{0,4},{1,5},{2,6},{3,7},{4,0},{5,1},{6,2},{7,3},{8,12},{9,13},{10,... | collective-permute-start | bytes 983048 | tf_op jit(solution)/shard_map/ppermute | solution.py:13
  56.4 7.4 collective-permute-start.3
  63.9 27.2 %collective-permute-start.4 = (f32[5,2,128,128]{3,2,1,0:T(8,128)S(1)}, f32[5,2,128,128]{3,2,1,0:T(8,128)S(1)}, u32[]{:S(2)}, u32[]{:S(2)}) collective-permute-start(f32[5,2,128,128]{3,2,1,0:T(8,128)S(1)} %maximum_select_fusion.3), channel_id=1, source_target_pairs={{0,16},{1,17},{2,18},{3,19},{4,20},{5,21},{6,22},{7,23},{8,24},{9,... | collective-permute-start | bytes 1966088 | tf_op jit(solution)/shard_map/ppermute | solution.py:13
  106.5 264.3 %all-reduce.8.cloned.1.call-start = ((), (), s32[]{:S(2)}) async-start(), calls=%async_computation | async-start | bytes 2621440 | tf_op jit(solution)/shard_map/psum | solution.py:101
  172.0 28.6 %copy-start.6 = (f32[640,128]{1,0:T(8,128)S(1)}, f32[640,128]{1,0:T(8,128)}, u32[]{:S(2)}) copy-start(f32[640,128]{1,0:T(8,128)} %get-tuple-element.6) | copy-start | bytes 983044
  172.0 7.6 collective-permute-start.5
  180.6 14.0 %collective-permute-start.6 = (f32[5,128,128]{2,1,0:T(8,128)S(1)}, f32[5,128,128]{2,1,0:T(8,128)S(1)}, u32[]{:S(2)}, u32[]{:S(2)}) collective-permute-start(f32[5,128,128]{2,1,0:T(8,128)S(1)} %broadcast_select_fusion.1), channel_id=1, source_target_pairs={{0,2},{1,3},{2,0},{3,1},{4,6},{5,7},{6,4},{7,5},{8,10},{9,11},{10,... | collective-permute-start | bytes 983048 | tf_op jit(solution)/shard_map/ppermute | solution.py:13
  194.7 19.7 %collective-permute-start.7 = (f32[5,128,128]{2,1,0:T(8,128)S(1)}, f32[5,128,128]{2,1,0:T(8,128)S(1)}, u32[]{:S(2)}, u32[]{:S(2)}) collective-permute-start(f32[5,128,128]{2,1,0:T(8,128)S(1)} %broadcast_select_fusion.4), channel_id=1, source_target_pairs={{0,4},{1,5},{2,6},{3,7},{4,0},{5,1},{6,2},{7,3},{8,12},{9,13},{10,... | collective-permute-start | bytes 983048 | tf_op jit(solution)/shard_map/ppermute | solution.py:13
  210.7 300.9 %all-reduce.14.cloned.1.call-start = ((), (), s32[]{:S(2)}) async-start(), calls=%async_computation.3 | async-start | bytes 1310720 | tf_op jit(solution)/shard_map/psum | solution.py:18
  214.4 19.8 %collective-permute-start.8 = (f32[5,1,128,128]{3,2,0,1:T(8,128)S(1)}, f32[5,1,128,128]{3,2,0,1:T(8,128)S(1)}, u32[]{:S(2)}, u32[]{:S(2)}) collective-permute-start(f32[5,1,128,128]{3,2,0,1:T(8,128)S(1)} %select_bitcast_fusion.1), channel_id=1, source_target_pairs={{0,8},{1,9},{2,10},{3,11},{4,12},{5,13},{6,14},{7,15},{8,0},{9,1},... | collective-permute-start | bytes 983048 | tf_op jit(solution)/shard_map/ppermute | solution.py:13
  234.3 25.5 %collective-permute-start.9 = (f32[5,2,128,128]{3,2,0,1:T(8,128)S(1)}, f32[5,2,128,128]{3,2,0,1:T(8,128)S(1)}, u32[]{:S(2)}, u32[]{:S(2)}) collective-permute-start(f32[5,2,128,128]{3,2,0,1:T(8,128)S(1)} %maximum_select_fusion.4), channel_id=1, source_target_pairs={{0,16},{1,17},{2,18},{3,19},{4,20},{5,21},{6,22},{7,23},{8,24},{9,... | collective-permute-start | bytes 1966088 | tf_op jit(solution)/shard_map/ppermute | solution.py:13
  372.2 2.3 copy-start.2
  431.5 15.4 %copy-start = (f32[20,128,128]{2,1,0:T(8,128)}, f32[20,128,128]{2,1,0:T(8,128)S(1)}, u32[]{:S(2)}) copy-start(f32[20,128,128]{2,1,0:T(8,128)S(1)} %convolution_add_fusion) | copy-start | bytes 3932164
  447.0 261.2 %all-reduce.10.cloned.1.call-start = ((), (), s32[]{:S(2)}) async-start(), calls=%async_computation.1 | async-start | bytes 2621440 | tf_op jit(solution)/shard_map/psum | solution.py:101
  511.6 28.5 %copy-start.5 = (f32[640,128]{1,0:T(8,128)S(1)}, f32[640,128]{1,0:T(8,128)}, u32[]{:S(2)}) copy-start(f32[640,128]{1,0:T(8,128)} %get-tuple-element.4) | copy-start | bytes 983044
  511.6 7.6 collective-permute-start.10
  520.2 13.6 %collective-permute-start.11 = (f32[5,128,128]{2,1,0:T(8,128)S(1)}, f32[5,128,128]{2,1,0:T(8,128)S(1)}, u32[]{:S(2)}, u32[]{:S(2)}) collective-permute-start(f32[5,128,128]{2,1,0:T(8,128)S(1)} %broadcast_select_fusion), channel_id=1, source_target_pairs={{0,2},{1,3},{2,0},{3,1},{4,6},{5,7},{6,4},{7,5},{8,10},{9,11},{10,... | collective-permute-start | bytes 983048 | tf_op jit(solution)/shard_map/ppermute | solution.py:13
  533.8 20.3 %collective-permute-start.12 = (f32[5,128,128]{2,1,0:T(8,128)S(1)}, f32[5,128,128]{2,1,0:T(8,128)}, u32[]{:S(2)}, u32[]{:S(2)}) collective-permute-start(f32[5,128,128]{2,1,0:T(8,128)S(1)} %broadcast_select_fusion.3), channel_id=1, source_target_pairs={{0,4},{1,5},{2,6},{3,7},{4,0},{5,1},{6,2},{7,3},{8,12},{9,13},{10,... | collective-permute-start | bytes 983048 | tf_op jit(solution)/shard_map/ppermute | solution.py:13
  550.3 270.0 %all-reduce.12.cloned.1.call-start = ((), (), s32[]{:S(2)}) async-start(), calls=%async_computation.2 | async-start | bytes 1310720 | tf_op jit(solution)/shard_map/psum | solution.py:18
  554.1 7.2 collective-permute-start.13
  561.3 18.6 %collective-permute-start.14 = (f32[5,2,128,128]{3,2,0,1:T(8,128)S(1)}, f32[5,2,128,128]{3,2,0,1:T(8,128)S(1)}, u32[]{:S(2)}, u32[]{:S(2)}) collective-permute-start(f32[5,2,128,128]{3,2,0,1:T(8,128)S(1)} %maximum_select_fusion.5), channel_id=1, source_target_pairs={{0,16},{1,17},{2,18},{3,19},{4,20},{5,21},{6,22},{7,23},{8,24},{9,... | collective-permute-start | bytes 1966088 | tf_op jit(solution)/shard_map/ppermute | solution.py:13
  708.1 2.1 copy-start.1
  749.7 2.7 copy-start.3
  749.7 2.7 copy-start.4
Sparse Core Ops, SparseCore 0:
  106.6 65.2 all-reduce.15
  210.8 159.9 all-reduce.7
  447.1 64.3 all-reduce.13
  550.4 157.7 all-reduce.9
  756.0 64.2 all-reduce.11
